TPU v7x, 512 devices: a whole 4x4x16 slice. The times are simulated.
512 devices in a mesh: seq: 32 (over y, z_lo), mp: 16 (over x, z_hi, core).
Axes of the slice: x: 4, y: 4, z: 16 (z_hi: 2, z_lo: 8; z = z_hi * 8 + z_lo), core: 2. Of those that a mesh axis runs over, the one named last changes fastest.
Arguments:
- tokens: bfloat16 [4096, 8192], P('seq', 'mp'), may hold values from -6 to 6
- in_weight: bfloat16 [8192, 3, 4096], P('seq', None, 'mp'), may hold values from -0.0625 to 0.0625
- short_taps: float32 [3, 3, 4096], P(None, None, 'mp'), may hold values from -4 to 4
- carry_rows: bfloat16 [2, 3, 4096], P(None, None, 'mp'), may hold values from -6 to 6
- pole_rates: float32 [16, 16], replicated, may hold values from 3e-05 to 0.03
- residues: float32 [16, 16], replicated, may hold values from -0.1 to 0.1
- carry_state: float32 [4096, 16], P('mp'), may hold values from -60 to 60
- skip_gain: float32 [4096], P('mp'), may hold values from -4 to 4
- groups: int32 [4096], P('mp'), may hold values from 0 to 15
Outputs:
- result: bfloat16 [4096, 4096], P('seq', 'mp')
All inputs are finite; a program needn't handle non-finite values.
Results may differ from a plain program's by a relative error of at most 0.008.
Values may be sent and summed in bfloat16 or wider, within the bound.
A program may use at most 128 MiB of HBM per device.

v0:
```python
import math

import jax
import jax.numpy as jnp
from jax import lax
from jax.sharding import PartitionSpec as P


def shifted(array, axis, by):
    length = lax.axis_size(axis)
    pairs = [(i, i + by) for i in range(length) if 0 <= i + by < length]
    return lax.ppermute(array, axis, pairs)


def project_rows(source, in_weight, out_width):
    gathered = lax.all_gather(source, "mp", axis=1, tiled=True)
    segment = lax.all_gather(in_weight, "seq", axis=0, tiled=True)
    return jnp.dot(
        gathered, segment.reshape(segment.shape[0], out_width), preferred_element_type=jnp.float32
    )


def channel_modes(chan_groups, pole_rates, residues):
    highest = lax.Precision.HIGHEST
    one_hot = (
        chan_groups[:, None] == jnp.arange(pole_rates.shape[0], dtype=jnp.int32)[None, :]
    ).astype(jnp.float32)
    chan_rates = jnp.dot(one_hot, pole_rates, precision=highest)
    chan_res = jnp.dot(one_hot, residues, precision=highest)
    return (chan_rates, chan_res)


def long_conv(signal, chan_rates, chan_res, chan_state, block_limit):
    highest = lax.Precision.HIGHEST
    chan_count, length = signal.shape
    block_len = math.gcd(length, block_limit)
    block_count = length // block_len
    steps_in = jnp.arange(block_len).astype(jnp.float32)
    decays = jnp.exp(-chan_rates[:, :, None] * steps_in)
    kernel = jnp.sum(chan_res[:, :, None] * decays, axis=1)
    lag_index = jnp.arange(block_len)[:, None] - jnp.arange(block_len)[None, :]
    toeplitz = jnp.where(lag_index >= 0, jnp.take(kernel, jnp.maximum(lag_index, 0), axis=1), 0.0)
    pieces = signal.reshape(chan_count, block_count, block_len)
    inner_part = jnp.einsum("cij,cnj->cni", toeplitz, pieces, precision=highest)
    tail_decay = jnp.exp(-chan_rates[:, :, None] * (block_len - 1.0 - steps_in))
    block_sums = jnp.einsum("crj,cnj->crn", tail_decay, pieces, precision=highest)
    index_blocks = jnp.arange(block_count)
    gap_steps = index_blocks[:, None] - 1 - index_blocks[None, :]
    gap_float = jnp.maximum(gap_steps, 0).astype(jnp.float32) * block_len
    transfer = jnp.where(gap_steps >= 0, jnp.exp(-chan_rates[:, :, None, None] * gap_float), 0.0)
    states = jnp.einsum("crnm,crm->crn", transfer, block_sums, precision=highest)
    start_decay = jnp.exp(-chan_rates[:, :, None] * (index_blocks.astype(jnp.float32) * block_len))
    states = states + start_decay * chan_state[:, :, None]
    lead_decay = chan_res[:, :, None] * jnp.exp(-chan_rates[:, :, None] * (steps_in + 1.0))
    outer_part = jnp.einsum("cri,crn->cni", lead_decay, states, precision=highest)
    return (inner_part + outer_part).reshape(chan_count, length)


def shards(
    tokens, in_weight, short_taps, carry_rows, pole_rates, residues, carry_state, skip_gain, groups
):
    row_count = tokens.shape[0]
    local_width = in_weight.shape[2]
    out_width = 3 * local_width
    is_first = lax.axis_index("seq") == 0
    projected = (
        project_rows(tokens, in_weight, out_width)
        .astype(jnp.bfloat16)
        .reshape(tokens.shape[0], 3, local_width)
    )
    head_rows = shifted(projected[row_count - 2 :], "seq", 1)
    head_rows = jnp.where(is_first, carry_rows, head_rows)
    extended = jnp.concatenate([head_rows, projected], axis=0).astype(jnp.float32)
    short_mix = (
        short_taps[0] * extended[2:]
        + short_taps[1] * extended[1:-1]
        + short_taps[2] * extended[:-2]
    )
    query_rows = short_mix[:, 0]
    gated_rows = (short_mix[:, 1] * short_mix[:, 2]).astype(jnp.bfloat16)
    channel_major = lax.all_to_all(gated_rows.T, "seq", split_axis=0, concat_axis=1, tiled=True)
    chan_count = channel_major.shape[0]
    offset = lax.axis_index("seq") * chan_count
    chan_groups = lax.dynamic_slice_in_dim(groups, offset, chan_count, 0)
    chan_state = lax.dynamic_slice_in_dim(carry_state, offset, chan_count, 0)
    chan_rates, chan_res = channel_modes(chan_groups, pole_rates, residues)
    long_mixed = long_conv(channel_major.astype(jnp.float32), chan_rates, chan_res, chan_state, 256)
    long_rows = lax.all_to_all(
        long_mixed.astype(jnp.bfloat16), "seq", split_axis=1, concat_axis=0, tiled=True
    ).T
    result = query_rows * (
        long_rows.astype(jnp.float32) + skip_gain * gated_rows.astype(jnp.float32)
    )
    return result.astype(jnp.bfloat16)


def solution(mesh):
    in_specs = (
        P("seq", "mp"),
        P("seq", None, "mp"),
        P(None, None, "mp"),
        P(None, None, "mp"),
        P(),
        P(),
        P("mp", None),
        P("mp"),
        P("mp"),
    )
    out_specs = P("seq", "mp")
    return jax.shard_map(shards, mesh=mesh, in_specs=in_specs, out_specs=out_specs, check_vma=False)
```

profile of v0, /device:TPU:7, one launch (start us, length us, event | category | flops | bytes accessed | tf_op | source)
XLA Modules:
  0.0 712.1 jit_solution(1981509274140765477)
XLA Ops:
  6.6 0.7 all-gather.3.cloned.1.call-update
  7.3 1.9 copy.25
  9.3 0.1 copy.37
  9.5 0.1 dynamic_slice.6
  9.6 0.1 constant_dynamic-slice_fusion
  9.7 0.2 convolution_negate_fusion
  9.9 0.2 fusion.41
  10.1 0.1 multiply_reduce_fusion
  10.2 0.1 fusion.40
  10.4 94.7 %all-gather.3.cloned.1.call-done = bf16[128,8192]{1,0:T(8,128)(2,1)} async-done(((bf16[128,512]{1,0:T(8,128)(2,1)}), bf16[128,8192]{1,0:T(8,128)(2,1)}) %all-gather.3.cloned.1.call-update) | async-done | bytes 2097168 | tf_op jit(solution)/shard_map/all_gather | solution.py:16
  105.1 308.8 %all-gather.5.cloned.1.call-done = bf16[8192,3,256]{0,2,1:T(8,128)(2,1)} async-done(((bf16[256,3,256]{0,2,1:T(8,128)(2,1)}), bf16[8192,3,256]{0,2,1:T(8,128)(2,1)}) %all-gather.5.cloned.1.call-update) | async-done | bytes 12582928 | tf_op jit(solution)/shard_map/all_gather | solution.py:17
  413.9 9.5 %convolution_convert_fusion = bf16[128,768]{1,0:T(8,128)(2,1)S(1)} fusion(bf16[128,8192]{1,0:T(8,128)(2,1)} %all-gather.3.cloned.1.call-done, bf16[8192,768]{0,1:T(8,128)(2,1)} %bitcast.52), kind=kOutput, calls=%fused_computation.5 | convolution fusion | flops 1610711040 | bytes 14876672 | tf_op jit(solution)/shard_map/dot_general | solution.py:18
  423.5 1.8 collective-permute-start
  425.3 0.2 copy.27
  425.4 0.6 collective-permute-done
  426.0 0.2 copy.28
  426.2 0.2 maximum_convert_fusion
  426.4 0.6 fusion.17
  427.0 0.6 fusion.56
  427.6 15.0 %all-to-all-start = ((bf16[32,8,128]{2,1,0:T(8,128)(2,1)}), bf16[32,8,128]{2,1,0:T(8,128)(2,1)S(1)}, u32[]{:S(2)}, u32[]{:S(2)}) async-start(bf16[32,8,128]{2,1,0:T(8,128)(2,1)} %fusion.56), calls=%async_computation | async-start | bytes 131072 | tf_op jit(solution)/shard_map/all_to_all | solution.py:81
  442.6 0.1 copy.30
  442.8 215.6 %gather_fusion = f32[65536,8]{1,0:T(8,128)} fusion(f32[8,256]{0,1:T(8,128)S(1)} %copy.30, s32[65536]{0:T(1024)S(1)} %broadcast_clamp_fusion), kind=kCustom, calls=%fused_computation | custom fusion | bytes 4456448 | tf_op jit(solution)/shard_map/jit(_take)/gather | solution.py:42
  658.4 18.6 %copy.31 = f32[256,256,8]{1,0,2:T(8,128)S(1)} copy(f32[256,256,8]{2,1,0:T(8,128)} %bitcast.51) | data formatting | bytes 4194304 | tf_op jit(solution)/shard_map/jit(_take)/gather | solution.py:42
  677.1 0.1 convert_multiply_fusion
  677.2 0.3 fusion.26
  677.5 1.9 fusion.7
  679.4 0.1 copy.36
  679.5 1.3 fusion
  680.8 0.3 fusion.4
  681.2 23.2 %all_to_all.26 = bf16[8,32,128]{2,0,1:T(8,128)(2,1)S(1)} all-to-all(bf16[8,32,128]{2,0,1:T(8,128)(2,1)S(1)} %copy.33), channel_id=1, replica_groups=mesh['seq'=32,'mp'=16] {'seq'}, dimensions={1} | all-to-all | bytes 131072 | tf_op jit(solution)/shard_map/all_to_all | solution.py:88
  704.4 0.1 fusion.22
  704.6 0.7 copy.34
  (35 shorter events, 0.5 us)
Async XLA Ops:
  6.5 3.0 copy-start
  6.5 2.9 copy-start.6
  6.5 3.2 copy-start.4
  6.5 3.4 copy-start.5
  6.5 3.8 copy-start.1
  6.5 98.5 %all-gather.3.cloned.1.call-start = ((), (), s32[]{:S(2)}) async-start(), calls=%async_computation.2 | async-start | bytes 2228224 | tf_op jit(solution)/shard_map/all_gather | solution.py:16
  7.3 406.6 %all-gather.5.cloned.1.call-start = ((), (), s32[]{:S(2)}) async-start(), calls=%async_computation.3 | async-start | bytes 12976128 | tf_op jit(solution)/shard_map/all_gather | solution.py:17
  413.9 12.1 %copy-start.2 = (bf16[2,3,256]{2,0,1:T(2,128)(2,1)S(1)}, bf16[2,3,256]{2,0,1:T(2,128)(2,1)}, u32[]{:S(2)}) copy-start(bf16[2,3,256]{2,0,1:T(2,128)(2,1)} %param.12) | copy-start | bytes 9220
  423.5 2.5 collective-permute-start
  427.6 249.5 %all-to-all-start = ((bf16[32,8,128]{2,1,0:T(8,128)(2,1)}), bf16[32,8,128]{2,1,0:T(8,128)(2,1)S(1)}, u32[]{:S(2)}, u32[]{:S(2)}) async-start(bf16[32,8,128]{2,1,0:T(8,128)(2,1)} %fusion.56), calls=%async_computation | async-start | bytes 131072 | tf_op jit(solution)/shard_map/all_to_all | solution.py:81
  677.5 27.0 %copy-start.3 = (f32[256]{0:T(256)S(1)}, f32[256]{0:T(256)}, u32[]{:S(2)}) copy-start(f32[256]{0:T(256)} %param.16) | copy-start | bytes 3076
Sparse Core Ops, SparseCore 0:
  10.5 94.5 all-gather.2
  107.1 306.7 all-gather.4
where the time goes:
time: 722 us; the launch traced here: 712 us
  waiting for transfers between devices  405 us (56%)
  local copies, waits for them, and re-layouts  238 us (33%)
  blocking collectives  23.2 us (3%)
  starting transfers between devices  16.9 us (2%)
  matrix products  13.7 us (2%)
  between operations  13.6 us (2%)
    all_gather x1, waiting for transfers between devices, project_rows(): segment = lax.all_gather(in_weight, 'seq', axis=0, tiled=True)  309 us
    gather x2, local copies, waits for them, and re-layouts, long_conv(): jnp.take(kernel, jnp.maximum(lag_index, 0), axis=1)  234 us
    all_gather x1, waiting for transfers between devices, project_rows(): gathered = lax.all_gather(source, 'mp', axis=1, tiled=True)  94.7 us
    all_to_all x1, blocking collectives, shards(): lax.all_to_all(long_mixed.astype(jnp.bfloat16), 'seq', split_axis=1, conc...  23.2 us
    all_to_all x1, starting transfers between devices, shards(): lax.all_to_all(gated_rows.T, 'seq', split_axis=0, concat_axis=1, tiled=True)  15 us
  transfers between devices with their start and end apart: 4, of which 3 were waited for; matrix products, arithmetic and copies ran while one was open for 33% of the time, Pallas kernels for 0%

commit v1 on v0

v1 whole, which is shorter than its diff:
```python
import functools

import jax
import jax.numpy as jnp
from jax import lax
from jax.experimental import pallas as pl
from jax.experimental.pallas import tpu as pltpu
from jax.sharding import PartitionSpec as P

MESH = pl.DeviceIdType.MESH
SUBS = 2
STAGE_TWO, SPREAD, FORWARD = 2, 5, 7


def device(x, y, z, c):
    return {"seq": y * 8 + z % 8, "mp": x * 4 + (z // 8) * 2 + c}


def kernel(
    tok_ref,
    w_ref,
    prm_ref,
    modes_ref,
    out_ref,
    a_buf,
    stage_buf,
    w_buf,
    part_buf,
    sum_buf,
    prm_buf,
    ext_buf,
    gated_buf,
    query_buf,
    long_buf,
    state_buf,
    halo_send,
    halo_recv,
    home_send,
    home_recv,
    ring_s,
    ring_r,
    sib_s,
    sib_r,
    one_s,
    one_r,
    two_s,
    two_r,
    col_s,
    col_r,
    sum_s,
    sum_r,
    st_s,
    st_r,
    misc_s,
    misc_r,
    home_s,
    home_r,
    local_sem,
):
    seq, mp = lax.axis_index("seq"), lax.axis_index("mp")
    y, zl = seq // 8, seq % 8
    x, zh, c = mp // 4, (mp // 2) % 2, mp % 2
    z = zh * 8 + zl

    def remote(src, dst, send, recv, to):
        return pltpu.make_async_remote_copy(
            src_ref=src,
            dst_ref=dst,
            send_sem=send,
            recv_sem=recv,
            device_id=to,
            device_id_type=MESH,
        )

    z_up, z_down = device(x, y, (z + 1) % 16, c), device(x, y, (z + 15) % 16, c)
    sibling = device(x, y, z, 1 - c)
    y_up, y_down = device(x, (y + 1) % 4, z, c), device(x, (y + 3) % 4, z, c)
    plane = [device((x + i % 4) % 4, (y + i // 4) % 4, z, c) for i in range(16)]
    turn = (zl + 8 - x - y) % 4
    one_to = [device(y, turn, z, h) for h in range(2)]
    one_from = [device(turn, x, z, h) for h in range(2)]
    two_to = [device(x, y, zh * 8 + 2 * turn + h, c) for h in range(2)]
    first = (zl // 2 + x + y) % 4
    two_from = [device(x, y, zh * 8 + first + 4 * h, c) for h in range(2)]
    home_z = zh * 8 + 2 * x
    home_to = [device(zl // 2, y, home_z + q, zl % 2) for q in range(2)]
    home_from = [device(zl // 2, y, home_z + c, h) for h in range(2)]
    partner = device(zl // 2, y, home_z + c, zl % 2)
    at_home = zl == 2 * x + c
    away = jnp.logical_not(at_home)
    one_same = jnp.logical_and(x == y, turn == y)

    barrier = pltpu.get_barrier_semaphore()
    met = [z_up, z_down, sibling] + plane[1:] + one_to + one_from + two_to + two_from
    met = met + home_to + home_from
    for other in met:
        pl.semaphore_signal(barrier, inc=1, device_id=other, device_id_type=MESH)
    pl.semaphore_wait(barrier, len(met))

    def one_copy(h):
        return remote(w_ref.at[h], stage_buf.at[c], one_s.at[h], one_r.at[c], one_to[h])

    for h in range(2):
        stays = jnp.logical_and(one_same, c == h)

        @pl.when(stays)
        def _():
            stage_buf[h] = w_ref[h]

        @pl.when(jnp.logical_not(stays))
        def _():
            one_copy(h).start()

    def wait_one():
        for h in range(2):

            @pl.when(jnp.logical_not(jnp.logical_and(one_same, c == h)))
            def _():
                remote(w_ref.at[h], stage_buf.at[h], one_s.at[h], one_r.at[h], one_to[h]).wait_recv()

    rows = 128 // SUBS

    def ring_copy(way, t, u):
        held = (z + 16 - t) % 16 if way == 0 else (z + t) % 16
        dst = a_buf.at[held, c, pl.ds(u * rows, rows)]
        src = tok_ref.at[pl.ds(u * rows, rows)] if t == 0 else dst
        return remote(
            src, dst, ring_s.at[way, t, u], ring_r.at[way, t, u], z_up if way == 0 else z_down
        )

    def sib_copy(way, t, u):
        held = (z + 16 - t) % 16 if way == 0 else (z + t) % 16
        dst = a_buf.at[held, c, pl.ds(u * rows, rows)]
        src = tok_ref.at[pl.ds(u * rows, rows)] if t == 0 else dst
        return remote(src, dst, sib_s.at[way, t, u], sib_r.at[way, t, u], sibling)

    def uses(way, t):
        if t < 7:
            return range(SUBS)
        return range(SUBS // 2) if way == 0 else range(SUBS // 2, SUBS)

    ring_sent, sib_sent = [], []
    for u in range(SUBS):
        for way in range(2):
            copy = ring_copy(way, 0, u)
            copy.start()
            ring_sent.append(copy)
    for u in range(SUBS):
        copy = sib_copy(0, 0, u)
        copy.start()
        sib_sent.append(copy)
    a_buf[z, c] = tok_ref[...]

    prm_copy = remote(prm_ref.at[zl % 2], prm_buf, misc_s.at[0], misc_r.at[0], partner)

    @pl.when(at_home)
    def _():
        prm_buf[...] = prm_ref[zl % 2]

    @pl.when(away)
    def _():
        prm_copy.start()

    def block(index):
        return w_buf.at[pl.ds(pl.multiple_of(index * 256, 256), 256)]

    def two_copy(h):
        return remote(stage_buf.at[h], block(zl), two_s.at[h], two_r.at[zl // 4], two_to[h])

    def two_stays(h):
        return zl == 2 * turn + h

    def send_two():
        for h in range(2):

            @pl.when(two_stays(h))
            def _():
                w_buf[pl.ds(pl.multiple_of(zl * 256, 256), 256), :] = stage_buf[h]

            @pl.when(jnp.logical_not(two_stays(h)))
            def _():
                two_copy(h).start()

    def wait_two():
        for h in range(2):

            @pl.when(zl != first + 4 * h)
            def _():
                remote(
                    stage_buf.at[h], block(first + 4 * h), two_s.at[h], two_r.at[h], two_to[h]
                ).wait_recv()

    def col_copy(way, hop, h):
        step = hop if way == 0 else -hop
        ref = block((first + 4 - step) % 4 + 4 * h)
        return remote(
            ref, ref, col_s.at[way, hop, h], col_r.at[way, hop, h], y_up if way == 0 else y_down
        )

    col_sent = []

    def spread():
        for h in range(2):
            for way in range(2):
                copy = col_copy(way, 0, h)
                copy.start()
                col_sent.append(copy)

    def forward():
        for way in range(2):
            col_copy(way, 0, way).wait_recv()
            copy = col_copy(way, 1, way)
            copy.start()
            col_sent.append(copy)

    for t in range(1, 9):
        for u in range(SUBS):
            for way in range(2):
                if u in uses(way, t - 1):
                    ring_copy(way, t - 1, u).wait_recv()
                    if t < 8 and u in uses(way, t):
                        copy = ring_copy(way, t, u)
                        copy.start()
                        ring_sent.append(copy)
                    copy = sib_copy(way, t, u)
                    copy.start()
                    sib_sent.append(copy)
        if t == STAGE_TWO:
            wait_one()
            send_two()
        if t == SPREAD:
            wait_two()
            spread()
        if t == FORWARD:
            forward()
    for way in range(2):
        col_copy(way, 0, 1 - way).wait_recv()
        col_copy(way, 1, way).wait_recv()
    for copy in sib_sent:
        copy.wait_recv()

    def sum_copy(k, r):
        to = r // 2
        return remote(
            part_buf.at[r],
            sum_buf.at[(x + 4 - to) % 4, r % 2],
            sum_s.at[k],
            sum_r.at[(x + 4 - to) % 4, r % 2],
            device(to, y, z, c),
        )

    def product(k, r):
        total = jnp.zeros((128, 384), jnp.float32)
        for half in range(2):
            for core in range(2):
                at = (half * 4 + core * 2) * 256
                total += jnp.dot(
                    a_buf[half * 8 + r, core],
                    w_buf[at : at + 512, :],
                    preferred_element_type=jnp.float32,
                )
        part_buf[r] = total.astype(jnp.bfloat16)

    def row_of(k):
        return (2 * x + 2 + k) % 8

    @pl.loop(0, 6)
    def _(k):
        r = row_of(k)
        product(k, r)
        sum_copy(k, r).start()

    @pl.loop(6, 8)
    def _(k):
        product(k, row_of(k))

    @pl.when(away)
    def _():
        prm_copy.wait_recv()

    groups = prm_buf[16:17, :]
    rates = jnp.zeros((16, 128), jnp.float32)
    res = jnp.zeros((16, 128), jnp.float32)
    for g in range(16):
        here = groups == float(g)
        rates = jnp.where(here, modes_ref[0:16, g : g + 1], rates)
        res = jnp.where(here, modes_ref[16:32, g : g + 1], res)
    decay = jnp.exp(-rates)
    decay_64 = jnp.exp(-64.0 * rates)
    decay_256 = jnp.exp(-256.0 * rates)

    for q in range(2):
        total = part_buf[2 * x + q].astype(jnp.float32)
        for i in range(1, 4):
            remote(
                part_buf.at[0], sum_buf.at[i, q], sum_s.at[0], sum_r.at[i, q], plane[1]
            ).wait_recv()
            total += sum_buf[i, q].astype(jnp.float32)
        rounded = total.astype(jnp.bfloat16)
        ext_buf[8 + 128 * q : 136 + 128 * q, :] = rounded.astype(jnp.float32)
        if q == 1:
            halo_send[...] = rounded[112:128, :]
    halo_copy = remote(
        halo_send,
        halo_recv,
        misc_s.at[1],
        misc_r.at[1],
        device((x + 1) % 4, (y + (x + 1) // 4) % 4, z, c),
    )
    halo_copy.start()
    halo_copy.wait_recv()
    is_first = jnp.logical_and(x == 0, y == 0)
    for i in range(2):
        for b in range(3):
            lanes = slice(128 * b, 128 * b + 128)
            row = halo_recv[:, lanes].astype(jnp.float32)[14 + i : 15 + i, :]
            carried = prm_buf[9 + 3 * i + b : 10 + 3 * i + b, :]
            ext_buf[6 + i : 7 + i, lanes] = jnp.where(is_first, carried, row)

    def mixed(b):
        lanes = slice(128 * b, 128 * b + 128)
        return (
            prm_buf[b : b + 1, :] * ext_buf[8:264, lanes]
            + prm_buf[3 + b : 4 + b, :] * ext_buf[7:263, lanes]
            + prm_buf[6 + b : 7 + b, :] * ext_buf[6:262, lanes]
        )

    query_buf[...] = mixed(0)
    gated_buf[...] = (mixed(1) * mixed(2)).astype(jnp.bfloat16).astype(jnp.float32)

    def leave(i, sums):
        return tuple(
            decay * s + jnp.broadcast_to(gated_buf[pl.ds(64 * k + i, 1), :], (16, 128))
            for k, s in enumerate(sums)
        )

    zero = jnp.zeros((16, 128), jnp.float32)
    sums = lax.fori_loop(0, 64, leave, (zero,) * 4)
    mine = 4 * y + x
    state_buf[mine] = sums[3] + decay_64 * (
        sums[2] + decay_64 * (sums[1] + decay_64 * sums[0])
    )

    def state_copy(i):
        return remote(
            state_buf.at[mine], state_buf.at[mine], st_s.at[i], st_r.at[i], plane[i]
        )

    for i in range(1, 16):
        state_copy(i).start()
    for i in range(1, 16):
        state_copy(i).wait_recv()
    state = prm_buf[24:40, :]
    for m in range(15):
        state = jnp.where(m < mine, decay_256 * state + state_buf[m], state)
    states = [state]
    for k in range(3):
        states.append(decay_64 * states[-1] + sums[k])

    def advance(i, held):
        new = []
        for k, s in enumerate(held):
            at = pl.ds(64 * k + i, 1)
            s = decay * s + jnp.broadcast_to(gated_buf[at, :], (16, 128))
            long_buf[at, :] = jnp.sum(res * s, axis=0, keepdims=True)
            new.append(s)
        return tuple(new)

    lax.fori_loop(0, 64, advance, tuple(states))

    long_rows = long_buf[...].astype(jnp.bfloat16).astype(jnp.float32)
    result = query_buf[...] * (long_rows + prm_buf[15:16, :] * gated_buf[...])
    result = result.astype(jnp.bfloat16)
    home_send[0] = result[0:128, :]
    home_send[1] = result[128:256, :]

    def home_copy(q):
        return remote(home_send.at[q], home_recv.at[c], home_s.at[q], home_r.at[c], home_to[q])

    for q in range(2):
        stays = jnp.logical_and(at_home, c == q)

        @pl.when(stays)
        def _():
            home_recv[q] = home_send[q]

        @pl.when(jnp.logical_not(stays))
        def _():
            home_copy(q).start()

    for copy in ring_sent + sib_sent + col_sent:
        copy.wait_send()
    for h in range(2):

        @pl.when(jnp.logical_not(jnp.logical_and(one_same, c == h)))
        def _():
            one_copy(h).wait_send()

        @pl.when(jnp.logical_not(two_stays(h)))
        def _():
            two_copy(h).wait_send()

    @pl.when(away)
    def _():
        prm_copy.wait_send()

    @pl.loop(0, 6)
    def _(k):
        sum_copy(k, row_of(k)).wait_send()

    halo_copy.wait_send()
    for i in range(1, 16):
        state_copy(i).wait_send()
    for q in range(2):

        @pl.when(jnp.logical_not(jnp.logical_and(at_home, c == q)))
        def _():
            home_copy(q).wait_send()
            remote(
                home_send.at[q], home_recv.at[q], home_s.at[q], home_r.at[q], home_to[q]
            ).wait_recv()

    for h in range(2):
        out_ref[:, 128 * h : 128 * h + 128] = home_recv[h]


def shards(
    tokens, in_weight, short_taps, carry_rows, pole_rates, residues, carry_state, skip_gain, groups
):
    depth = in_weight.shape[0]
    weight = in_weight.reshape(depth, 3, 2, 128).transpose(2, 0, 1, 3).reshape(2, depth, 384)
    width = skip_gain.shape[0]
    packed = jnp.concatenate(
        [
            short_taps.reshape(9, width),
            carry_rows.astype(jnp.float32).reshape(6, width),
            skip_gain[None],
            groups.astype(jnp.float32)[None],
            jnp.zeros((7, width), jnp.float32),
            carry_state.T,
        ],
        axis=0,
    )
    packed = packed.reshape(40, 2, 128).transpose(1, 0, 2)
    modes = jnp.concatenate([pole_rates.T, residues.T], axis=0)
    vmem = pl.BlockSpec(memory_space=pltpu.VMEM)
    dma = pltpu.SemaphoreType.DMA
    return pl.pallas_call(
        kernel,
        out_shape=jax.ShapeDtypeStruct((128, 256), jnp.bfloat16),
        in_specs=[vmem] * 4,
        out_specs=vmem,
        scratch_shapes=[
            pltpu.VMEM((16, 2, 128, 512), jnp.bfloat16),
            pltpu.VMEM((2, 256, 384), jnp.bfloat16),
            pltpu.VMEM((2048, 384), jnp.bfloat16),
            pltpu.VMEM((8, 128, 384), jnp.bfloat16),
            pltpu.VMEM((4, 2, 128, 384), jnp.bfloat16),
            pltpu.VMEM((40, 128), jnp.float32),
            pltpu.VMEM((264, 384), jnp.float32),
            pltpu.VMEM((256, 128), jnp.float32),
            pltpu.VMEM((256, 128), jnp.float32),
            pltpu.VMEM((256, 128), jnp.float32),
            pltpu.VMEM((16, 16, 128), jnp.float32),
            pltpu.VMEM((16, 384), jnp.bfloat16),
            pltpu.VMEM((16, 384), jnp.bfloat16),
            pltpu.VMEM((2, 128, 128), jnp.bfloat16),
            pltpu.VMEM((2, 128, 128), jnp.bfloat16),
            dma((2, 8, SUBS)),
            dma((2, 8, SUBS)),
            dma((2, 9, SUBS)),
            dma((2, 9, SUBS)),
            dma((2,)),
            dma((2,)),
            dma((2,)),
            dma((2,)),
            dma((2, 2, 2)),
            dma((2, 2, 2)),
            dma((8,)),
            dma((4, 2)),
            dma((16,)),
            dma((16,)),
            dma((2,)),
            dma((2,)),
            dma((2,)),
            dma((2,)),
            dma,
        ],
        compiler_params=pltpu.CompilerParams(
            collective_id=0, has_side_effects=True, vmem_limit_bytes=40 * 1024 * 1024
        ),
        name="operator",
    )(tokens, weight, packed, modes)


def solution(mesh):
    in_specs = (
        P("seq", "mp"),
        P("seq", None, "mp"),
        P(None, None, "mp"),
        P(None, None, "mp"),
        P(),
        P(),
        P("mp", None),
        P("mp"),
        P("mp"),
    )
    out_specs = P("seq", "mp")
    return jax.shard_map(shards, mesh=mesh, in_specs=in_specs, out_specs=out_specs, check_vma=False)
```

time: 722 us -> 105 us (0.15)
  the two profiles are of different devices: /device:TPU:7 before, /device:TPU:2 now
where the time goes in v1:
time: 105 us
  Pallas kernels  100 us (95%)
  local copies, waits for them, and re-layouts  4.71 us (4%)
    pallas_call x1, Pallas kernels, shards(): pl.pallas_call(kernel, out_shape=jax.ShapeDtypeStruct((128, 256), jnp.bfl...  100 us
    unnamed x20, local copies, waits for them, and re-layouts  4.37 us

profile of v1, /device:TPU:2, one launch (start us, length us, event | category | flops | bytes accessed | tf_op | source)
XLA Modules:
  0.0 105.2 jit_solution(11931434323101613855)
XLA Ops:
  0.0 0.0 copy-start
  0.0 1.2 %copy.20 = bf16[256,3,256]{0,2,1:T(8,128)(2,1)S(1)} copy(bf16[256,3,256]{2,0,1:T(8,128)(2,1)} %param.10) | data formatting | bytes 786432 | tf_op args[1]
  1.2 0.0 copy-start.2
  1.2 0.2 copy.28.w_ref
  1.4 0.5 copy-done.2
  1.9 0.0 copy-start.5
  2.0 0.0 copy-start.7
  2.0 0.0 copy-start.6
  2.0 0.6 copy-done.5
  2.6 0.0 copy-start.1
  2.7 0.0 copy-done
  2.7 0.0 copy-done.7
  2.7 0.0 copy-done.6
  2.7 0.0 copy-start.3
  2.8 0.6 copy-done.3
  3.4 0.0 copy-start.4
  3.4 0.1 copy.26
  3.5 0.6 copy-done.4
  4.1 0.1 copy.27
  4.2 0.0 copy-done.1
  4.2 100.3 %operator.1 = bf16[128,256]{1,0:T(8,128)(2,1)S(1)} custom-call(bf16[128,512]{1,0:T(8,128)(2,1)S(1)} %copy-done.1, bf16[2,256,384]{2,1,0:T(8,128)(2,1)S(1)} %copy.28.w_ref, f32[2,40,128]{2,1,0:T(8,128)S(1)} %bitcast.15, f32[32,16]{1,0:T(8,128)S(1)} %pad_maximum_fusion.modes_ref), custom_call_target="tpu_custom_call" | custom-call | tf_op jit(solution)/shard_map/operator/pallas_call | solution.py:448
  104.6 0.6 copy.32
  (11 shorter events, 0.1 us)
Async XLA Ops:
  0.0 2.7 %copy-start = (f32[256,16]{0,1:T(8,128)S(1)}, f32[256,16]{0,1:T(8,128)}, u32[]{:S(2)}) copy-start(f32[256,16]{0,1:T(8,128)} %param.15) | copy-start | bytes 49156
  1.2 0.7 copy-start.2
  1.9 0.7 copy-start.5
  2.0 0.7 copy-start.7
  2.0 0.7 copy-start.6
  2.6 1.6 %copy-start.1 = (bf16[128,512]{1,0:T(8,128)(2,1)S(1)}, bf16[128,512]{1,0:T(8,128)(2,1)}, u32[]{:S(2)}) copy-start(bf16[128,512]{1,0:T(8,128)(2,1)} %tok_ref.1) | copy-start | bytes 393220
  2.7 0.7 copy-start.3
  3.4 0.7 copy-start.4

commit v2 on v0

v2 whole, which is shorter than its diff:
```python
import jax
import jax.numpy as jnp
from jax import lax
from jax.experimental import pallas as pl
from jax.experimental.pallas import tpu as pltpu
from jax.sharding import PartitionSpec as P

MESH = pl.DeviceIdType.MESH
SUBS = 4
MOVE, SPREAD, FORWARD = (2, 8), (4, 9), (6, 10)
BRANCHES = ((1, 2), (0, 1))


def device(x, y, z, c):
    return {"seq": y * 8 + z % 8, "mp": x * 4 + (z // 8) * 2 + c}


def kernel(
    tok_in,
    w_in,
    taps_in,
    carry_in,
    pole_in,
    res_in,
    start_in,
    skip_in,
    group_in,
    out_ref,
    tok_ref,
    w_ref,
    taps_ref,
    carry_ref,
    pole_ref,
    res_ref,
    start_ref,
    skip_ref,
    group_ref,
    a_buf,
    stage_buf,
    w_buf,
    part_kv,
    part_q,
    sum_kv,
    sum_q,
    prm_send,
    prm_buf,
    turn_buf,
    mode_buf,
    ext_buf,
    gated_buf,
    long_buf,
    state_buf,
    halo_send,
    halo_recv,
    home_send,
    home_recv,
    ring_s,
    ring_r,
    sib_s,
    sib_r,
    one_s,
    one_r,
    two_s,
    two_r,
    col_s,
    col_r,
    sum_s,
    sum_r,
    st_s,
    st_r,
    prm_s,
    prm_r,
    halo_s,
    halo_r,
    home_s,
    home_r,
    in_s,
):
    taken = [
        pltpu.make_async_copy(src, dst, in_s.at[i])
        for i, (src, dst) in enumerate(
            (
                (tok_in, tok_ref),
                (w_in, w_ref),
                (taps_in, taps_ref),
                (carry_in, carry_ref),
                (pole_in, pole_ref),
                (res_in, res_ref),
                (start_in, start_ref),
                (skip_in, skip_ref),
                (group_in, group_ref),
            )
        )
    ]
    for copy in taken:
        copy.start()
    seq, mp = lax.axis_index("seq"), lax.axis_index("mp")
    y, zl = seq // 8, seq % 8
    x, zh, c = mp // 4, (mp // 2) % 2, mp % 2
    z = zh * 8 + zl

    def remote(src, dst, send, recv, to):
        return pltpu.make_async_remote_copy(
            src_ref=src,
            dst_ref=dst,
            send_sem=send,
            recv_sem=recv,
            device_id=to,
            device_id_type=MESH,
        )

    z_up, z_down = device(x, y, (z + 1) % 16, c), device(x, y, (z + 15) % 16, c)
    sibling = device(x, y, z, 1 - c)
    y_up, y_down = device(x, (y + 1) % 4, z, c), device(x, (y + 3) % 4, z, c)
    plane = [device((x + i % 4) % 4, (y + i // 4) % 4, z, c) for i in range(16)]
    turn = (zl + 8 - x - y) % 4
    one_to = [device(y, turn, z, h) for h in range(2)]
    one_from = [device(turn, x, z, h) for h in range(2)]
    two_to = [device(x, y, zh * 8 + 2 * turn + h, c) for h in range(2)]
    first = (zl // 2 + x + y) % 4
    two_from = [device(x, y, zh * 8 + first + 4 * h, c) for h in range(2)]
    own = (x + zl // 2) % 4
    home_to = [device(zl // 2, y, zh * 8 + 2 * own + q, zl % 2) for q in range(2)]
    owner = (zl // 2 + 4 - x) % 4
    home_from = [device(owner, y, zh * 8 + 2 * x + c, h) for h in range(2)]
    partner = device(owner, y, zh * 8 + 2 * x + c, zl % 2)
    at_home = jnp.logical_and(zl // 2 == x, zl == 2 * own + c)
    away = jnp.logical_not(at_home)
    one_same = jnp.logical_and(x == y, turn == y)

    barrier = pltpu.get_barrier_semaphore()
    met = [z_up, z_down, sibling] + plane[1:] + one_to + one_from + two_to + two_from
    met = met + home_to + home_from
    for other in met:
        pl.semaphore_signal(barrier, inc=1, device_id=other, device_id_type=MESH)

    for copy in taken:
        copy.wait()

    def half(rows):
        return jnp.where(zl % 2 == 0, rows[:, 0:128], rows[:, 128:256])

    for tap in range(3):
        prm_send[3 * tap : 3 * tap + 3, :] = half(taps_ref[tap])
    for b in range(3):
        pair = half(carry_ref[b].astype(jnp.float32))
        for i in range(2):
            prm_send[9 + 3 * i + b : 10 + 3 * i + b, :] = pair[i : i + 1, :]
    prm_send[15:16, :] = half(skip_ref[...])
    prm_send[16:17, :] = half(group_ref[...].astype(jnp.float32))
    prm_send[17:24, :] = jnp.zeros((7, 128), jnp.float32)
    prm_send[24:40, :] = half(start_ref[...])
    turn_buf[...] = jnp.zeros((128, 128), jnp.float32)
    turn_buf[0:16, 0:16] = pole_ref[...]
    turn_buf[16:32, 0:16] = res_ref[...]
    turn_buf[...] = jnp.transpose(turn_buf[...])

    pl.semaphore_wait(barrier, len(met))

    def one_copy(h, p, landed=None):
        some = pl.ds(*BRANCHES[p])
        at = c if landed is None else landed
        src = w_ref.at[some, :, pl.ds(h * 128, 128)]
        return remote(src, stage_buf.at[at, some], one_s.at[h, p], one_r.at[at, p], one_to[h])

    def one_stays(h):
        return jnp.logical_and(one_same, c == h)

    def set_out(p):
        for h in range(2):

            @pl.when(jnp.logical_not(one_stays(h)))
            def _():
                one_copy(h, p).start()

    set_out(0)

    rows = 128 // SUBS

    def held(way, t):
        return (z + 16 - t) % 16 if way == 0 else (z + t) % 16

    def ring_copy(way, t, u):
        part = pl.ds(u * rows, rows)
        dst = a_buf.at[held(way, t), c, part]
        src = tok_ref.at[part] if t == 0 else dst
        to = z_up if way == 0 else z_down
        return remote(src, dst, ring_s.at[way, t, u], ring_r.at[way, t, u], to)

    def sib_copy(way, t):
        part = pl.ds(0, 128) if t < 8 else pl.ds(64 * way, 64)
        dst = a_buf.at[held(way, t), c, part]
        src = tok_ref if t == 0 else dst
        return remote(src, dst, sib_s.at[way, t], sib_r.at[way, t], sibling)

    def uses(way, t):
        if t < 7:
            return range(SUBS)
        return range(SUBS // 2) if way == 0 else range(SUBS // 2, SUBS)

    sent, sib_sent = [], []
    for u in range(SUBS):
        for way in range(2):
            copy = ring_copy(way, 0, u)
            copy.start()
            sent.append(copy)
    copy = sib_copy(0, 0)
    copy.start()
    sib_sent.append(copy)

    prm_copy = remote(prm_send, prm_buf, prm_s.at[0], prm_r.at[0], partner)

    @pl.when(away)
    def _():
        prm_copy.start()

    @pl.when(at_home)
    def _():
        prm_buf[...] = prm_send[...]

    a_buf[z, c] = tok_ref[...]
    for h in range(2):

        @pl.when(one_stays(h))
        def _():
            stage_buf[h] = w_ref[:, :, h * 128 : h * 128 + 128]

    def block(index, p):
        at = pl.ds(pl.multiple_of(index * 256, 256), 256)
        return w_buf.at[pl.ds(*BRANCHES[p]), at]

    def two_copy(h, p):
        src = stage_buf.at[h, pl.ds(*BRANCHES[p])]
        return remote(src, block(zl, p), two_s.at[h, p], two_r.at[zl // 4, p], two_to[h])

    def two_stays(h):
        return zl == 2 * turn + h

    def move(h, p):
        @pl.when(jnp.logical_not(one_stays(h)))
        def _():
            one_copy(h, p, h).wait_recv()

        @pl.when(two_stays(h))
        def _():
            low, count = BRANCHES[p]
            at = pl.ds(pl.multiple_of(zl * 256, 256), 256)
            for b in range(low, low + count):
                w_buf[b, at, :] = stage_buf[h, b]

        @pl.when(jnp.logical_not(two_stays(h)))
        def _():
            two_copy(h, p).start()

    def col_copy(way, hop, h, p):
        step = hop if way == 0 else -hop
        ref = block((first + 4 - step) % 4 + 4 * h, p)
        to = y_up if way == 0 else y_down
        return remote(ref, ref, col_s.at[way, hop, h, p], col_r.at[way, hop, h, p], to)

    def spread(h, p):
        @pl.when(zl != first + 4 * h)
        def _():
            src = stage_buf.at[h, pl.ds(*BRANCHES[p])]
            dst = block(first + 4 * h, p)
            remote(src, dst, two_s.at[h, p], two_r.at[h, p], two_to[h]).wait_recv()

        for way in range(2):
            copy = col_copy(way, 0, h, p)
            copy.start()
            sent.append(copy)

    def forward(way, p):
        col_copy(way, 0, way, p).wait_recv()
        copy = col_copy(way, 1, way, p)
        copy.start()
        sent.append(copy)

    def gathered(p):
        for way in range(2):
            col_copy(way, 0, 1 - way, p).wait_recv()
            col_copy(way, 1, way, p).wait_recv()

    def weights_at(t):
        for p in range(2):
            for h in range(2):
                if t == MOVE[p]:
                    move(h, p)
            if t == MOVE[0] and p == 0:
                set_out(1)
            for h in range(2):
                if t == SPREAD[p]:
                    spread(h, p)
            for h in range(2):
                if t == FORWARD[p]:
                    forward(h, p)

    def modes():
        @pl.when(away)
        def _():
            prm_copy.wait_recv()

        groups = prm_buf[16:17, :]
        rates = jnp.zeros((16, 128), jnp.float32)
        res = jnp.zeros((16, 128), jnp.float32)
        for g in range(16):
            here = groups == float(g)
            rates = jnp.where(here, turn_buf[0:16, g : g + 1], rates)
            res = jnp.where(here, turn_buf[0:16, 16 + g : 17 + g], res)
        mode_buf[0] = jnp.exp(-rates)
        mode_buf[1] = jnp.exp(-64.0 * rates)
        mode_buf[2] = jnp.exp(-256.0 * rates)
        mode_buf[3] = res

    for t in range(1, 9):
        for u in range(SUBS):
            for way in range(2):
                if u in uses(way, t - 1):
                    ring_copy(way, t - 1, u).wait_recv()
                    if t < 8 and u in uses(way, t):
                        copy = ring_copy(way, t, u)
                        copy.start()
                        sent.append(copy)
        for way in range(2):
            copy = sib_copy(way, t)
            copy.start()
            sib_sent.append(copy)
        weights_at(t)
        if t == 5:
            modes()
    gathered(0)
    for copy in sib_sent:
        copy.wait_recv()

    def sum_copy(p, k):
        part, to_buf = ((part_kv, sum_kv), (part_q, sum_q))[p]
        to = (x + 1 + k) % 4
        return remote(
            part.at[k], to_buf.at[k], sum_s.at[p, k], sum_r.at[p, k], device(to, y, z, c)
        )

    def product(p, to):
        total = None
        for side in range(2):
            for core in range(2):
                at = slice((side * 4 + core * 2) * 256, (side * 4 + core * 2) * 256 + 512)
                left = a_buf[pl.ds(side * 8 + 2 * ((to + zl // 2) % 4), 2), core].reshape(256, 512)
                if p == 0:
                    right = jnp.concatenate([w_buf[1, at, :], w_buf[2, at, :]], axis=1)
                else:
                    right = w_buf[0, at, :]
                term = jnp.dot(left, right, preferred_element_type=jnp.float32)
                total = term if total is None else total + term
        return total

    lanes_of = (slice(128, 384), slice(0, 128))

    def products(p):
        part = (part_kv, part_q)[p]

        @pl.loop(0, 3)
        def _(k):
            part[k] = product(p, (x + 1 + k) % 4).astype(jnp.bfloat16)
            sum_copy(p, k).start()

        ext_buf[8:264, lanes_of[p]] = product(p, x)

    halo_to = device((x + 1) % 4, (y + (own + 1) // 4) % 4, z, c)
    is_first = jnp.logical_and(own == 0, y == 0)

    def halo_copy(p):
        part = pl.ds(lanes_of[p].start, lanes_of[p].stop - lanes_of[p].start)
        return remote(
            halo_send.at[:, part], halo_recv.at[:, part], halo_s.at[p], halo_r.at[p], halo_to
        )

    def collect(p):
        got = (sum_kv, sum_q)[p]
        total = ext_buf[8:264, lanes_of[p]]
        for k in range(3):
            sum_copy(p, k).wait_recv()
            total += got[k].astype(jnp.float32)
        rounded = total.astype(jnp.bfloat16)
        halo_send[:, lanes_of[p]] = rounded[240:256, :]
        halo_copy(p).start()
        ext_buf[8:264, lanes_of[p]] = rounded.astype(jnp.float32)

    def join(p):
        halo_copy(p).wait_recv()
        low, count = BRANCHES[p]
        for b in range(low, low + count):
            lanes = slice(128 * b, 128 * b + 128)
            last = halo_recv[:, lanes].astype(jnp.float32)
            for i in range(2):
                carried = prm_buf[9 + 3 * i + b : 10 + 3 * i + b, :]
                ext_buf[6 + i : 7 + i, lanes] = jnp.where(
                    is_first, carried, last[14 + i : 15 + i, :]
                )

    def mixed(b):
        lanes = slice(128 * b, 128 * b + 128)
        return (
            prm_buf[b : b + 1, :] * ext_buf[8:264, lanes]
            + prm_buf[3 + b : 4 + b, :] * ext_buf[7:263, lanes]
            + prm_buf[6 + b : 7 + b, :] * ext_buf[6:262, lanes]
        )

    products(0)
    weights_at(8 + 1)
    collect(0)
    join(0)
    gated_buf[...] = (mixed(1) * mixed(2)).astype(jnp.bfloat16).astype(jnp.float32)

    decay, decay_64, decay_256, res = [mode_buf[i] for i in range(4)]

    def leave(i, sums):
        new = []
        for k, s in enumerate(sums):
            some = gated_buf[pl.ds(pl.multiple_of(64 * k + 8 * i, 8), 8), :]
            for j in range(8):
                s = decay * s + jnp.broadcast_to(some[j : j + 1, :], (16, 128))
            new.append(s)
        return tuple(new)

    zero = jnp.zeros((16, 128), jnp.float32)
    sums = lax.fori_loop(0, 8, leave, (zero,) * 4)
    mine = 4 * y + own
    state_buf[mine] = sums[3] + decay_64 * (
        sums[2] + decay_64 * (sums[1] + decay_64 * sums[0])
    )

    def state_copy(i):
        here = state_buf.at[mine]
        return remote(here, here, st_s.at[i], st_r.at[i], plane[i])

    for i in range(1, 16):
        state_copy(i).start()

    weights_at(8 + 2)
    gathered(1)
    products(1)

    for i in range(1, 16):
        state_copy(i).wait_recv()
    state = prm_buf[24:40, :]
    for m in range(15):
        state = jnp.where(m < mine, decay_256 * state + state_buf[m], state)
    states = [state]
    for k in range(3):
        states.append(decay_64 * states[-1] + sums[k])
    collect(1)

    def advance(i, held_states):
        new = []
        for k, s in enumerate(held_states):
            at = pl.ds(pl.multiple_of(64 * k + 8 * i, 8), 8)
            some = gated_buf[at, :]
            out = []
            for j in range(8):
                s = decay * s + jnp.broadcast_to(some[j : j + 1, :], (16, 128))
                out.append(jnp.sum(res * s, axis=0, keepdims=True))
            long_buf[at, :] = jnp.concatenate(out, axis=0)
            new.append(s)
        return tuple(new)

    lax.fori_loop(0, 8, advance, tuple(states))

    join(1)
    long_rows = long_buf[...].astype(jnp.bfloat16).astype(jnp.float32)
    result = mixed(0) * (long_rows + prm_buf[15:16, :] * gated_buf[...])
    result = result.astype(jnp.bfloat16)
    home_send[0] = result[0:128, :]
    home_send[1] = result[128:256, :]

    def home_copy(q):
        return remote(home_send.at[q], home_recv.at[c], home_s.at[q], home_r.at[c], home_to[q])

    for q in range(2):
        stays = jnp.logical_and(at_home, c == q)

        @pl.when(stays)
        def _():
            home_recv[q] = home_send[q]

        @pl.when(jnp.logical_not(stays))
        def _():
            home_copy(q).start()

    for copy in sent + sib_sent:
        copy.wait_send()
    for p in range(2):
        for h in range(2):

            @pl.when(jnp.logical_not(one_stays(h)))
            def _():
                one_copy(h, p).wait_send()

            @pl.when(jnp.logical_not(two_stays(h)))
            def _():
                two_copy(h, p).wait_send()

        for k in range(3):
            sum_copy(p, k).wait_send()
        halo_copy(p).wait_send()

    @pl.when(away)
    def _():
        prm_copy.wait_send()

    for i in range(1, 16):
        state_copy(i).wait_send()
    for q in range(2):

        @pl.when(jnp.logical_not(jnp.logical_and(at_home, c == q)))
        def _():
            home_copy(q).wait_send()
            remote(
                home_send.at[q], home_recv.at[q], home_s.at[q], home_r.at[q], home_to[q]
            ).wait_recv()

    for h in range(2):
        out_ref[:, 128 * h : 128 * h + 128] = home_recv[h]


def shards(
    tokens, in_weight, short_taps, carry_rows, pole_rates, residues, carry_state, skip_gain, groups
):
    vmem = pl.BlockSpec(memory_space=pltpu.VMEM)
    dma = pltpu.SemaphoreType.DMA
    bf16, f32 = jnp.bfloat16, jnp.float32
    operands = (
        tokens,
        in_weight.transpose(1, 0, 2),
        short_taps,
        carry_rows.transpose(1, 0, 2),
        pole_rates,
        residues,
        carry_state.T,
        skip_gain[None],
        groups[None],
    )
    return pl.pallas_call(
        kernel,
        out_shape=jax.ShapeDtypeStruct((128, 256), bf16),
        in_specs=[pl.BlockSpec(memory_space=pl.ANY)] * 9,
        out_specs=vmem,
        scratch_shapes=[pltpu.VMEM(a.shape, a.dtype) for a in operands]
        + [
            pltpu.VMEM((16, 2, 128, 512), bf16),
            pltpu.VMEM((2, 3, 256, 128), bf16),
            pltpu.VMEM((3, 2048, 128), bf16),
            pltpu.VMEM((3, 256, 256), bf16),
            pltpu.VMEM((3, 256, 128), bf16),
            pltpu.VMEM((3, 256, 256), bf16),
            pltpu.VMEM((3, 256, 128), bf16),
            pltpu.VMEM((40, 128), f32),
            pltpu.VMEM((40, 128), f32),
            pltpu.VMEM((128, 128), f32),
            pltpu.VMEM((4, 16, 128), f32),
            pltpu.VMEM((264, 384), f32),
            pltpu.VMEM((256, 128), f32),
            pltpu.VMEM((256, 128), f32),
            pltpu.VMEM((16, 16, 128), f32),
            pltpu.VMEM((16, 384), bf16),
            pltpu.VMEM((16, 384), bf16),
            pltpu.VMEM((2, 128, 128), bf16),
            pltpu.VMEM((2, 128, 128), bf16),
            dma((2, 8, SUBS)),
            dma((2, 8, SUBS)),
            dma((2, 9)),
            dma((2, 9)),
            dma((2, 2)),
            dma((2, 2)),
            dma((2, 2)),
            dma((2, 2)),
            dma((2, 2, 2, 2)),
            dma((2, 2, 2, 2)),
            dma((2, 3)),
            dma((2, 3)),
            dma((16,)),
            dma((16,)),
            dma((1,)),
            dma((1,)),
            dma((2,)),
            dma((2,)),
            dma((2,)),
            dma((2,)),
            dma((9,)),
        ],
        compiler_params=pltpu.CompilerParams(
            collective_id=0, has_side_effects=True, vmem_limit_bytes=63 * 1024 * 1024
        ),
        name="operator",
    )(*operands)


def solution(mesh):
    in_specs = (
        P("seq", "mp"),
        P("seq", None, "mp"),
        P(None, None, "mp"),
        P(None, None, "mp"),
        P(),
        P(),
        P("mp", None),
        P("mp"),
        P("mp"),
    )
    out_specs = P("seq", "mp")
    return jax.shard_map(shards, mesh=mesh, in_specs=in_specs, out_specs=out_specs, check_vma=False)
```

time: 722 us -> 94.4 us (0.13); the launches traced: 712 us -> 94.2 us
  waiting for transfers between devices: 405 us -> 0 us
  local copies, waits for them, and re-layouts: 238 us -> 1.47 us
  Pallas kernels: 0 us -> 92.8 us
  blocking collectives: 23.2 us -> 0 us
  starting transfers between devices: 16.9 us -> 0 us
  matrix products: 13.7 us -> 0 us
  between operations: 13.6 us -> 0.01 us
    all_gather x2 -> x0, waiting for transfers between devices: 404 us -> none  [the longest x1 309 us: project_rows(): segment = lax.all_gather(in_weight, 'seq', axis=0, tiled=True)]
    gather x2 -> x0, local copies, waits for them, and re-layouts: 234 us -> none  [long_conv(): jnp.take(kernel, jnp.maximum(lag_index, 0), axis=1)]
    pallas_call x0 -> x1, Pallas kernels: none -> 92.8 us  [shards(): pl.pallas_call(kernel, out_shape=jax.ShapeDtypeStruct((128, 256), bf16),...]
    all_to_all x1 -> x0, blocking collectives: 23.2 us -> none  [shards(): lax.all_to_all(long_mixed.astype(jnp.bfloat16), 'seq', split_axis=1, conc...]
    all_to_all x1 -> x0, starting transfers between devices: 15 us -> none  [shards(): lax.all_to_all(gated_rows.T, 'seq', split_axis=0, concat_axis=1, tiled=True)]
    dot_general x7 -> x0, matrix products: 13.7 us -> none  [the longest x1 9.5 us: project_rows(): jnp.dot(gathered, segment.reshape(segment.shape[0], out_width), preferred...]
  transfers between devices with their start and end apart: 4 -> 0, of which waited for: 3 -> 0; matrix products, arithmetic and copies ran while one was open for 33% -> 0% of each run, Pallas kernels for 0% -> 0%
where the time goes in v2:
time: 94.4 us; the launch traced here: 94.2 us
  Pallas kernels  92.8 us (98%)
  local copies, waits for them, and re-layouts  1.47 us (2%)
    pallas_call x1, Pallas kernels, shards(): pl.pallas_call(kernel, out_shape=jax.ShapeDtypeStruct((128, 256), bf16),...  92.8 us

profile of v2, /device:TPU:7, one launch (start us, length us, event | category | flops | bytes accessed | tf_op | source)
XLA Modules:
  0.0 94.2 jit_solution(16865770250199099617)
XLA Ops:
  0.0 92.8 %operator.1 = bf16[128,256]{1,0:T(8,128)(2,1)} custom-call(bf16[128,512]{1,0:T(8,128)(2,1)} %tok_in.1, bf16[3,256,256]{2,1,0:T(8,128)(2,1)} %bitcast.5, f32[3,3,256]{2,1,0:T(4,128)} %taps_in.1, bf16[3,2,256]{2,1,0:T(2,128)(2,1)} %bitcast.7, f32[16,16]{1,0:T(8,128)} %pole_in.1, f32[16,16]{1,0:T(8,128)} %res_in.1, f32[16,256]{1,0:T(8,128)} %bitcast.6, ...), custom_call_target="tpu_custom_call" | custom-call | tf_op jit(solution)/shard_map/operator/pallas_call | solution.py:542
  92.8 1.5 %copy.11 = bf16[128,256]{1,0:T(8,128)(2,1)} copy(bf16[128,256]{1,0:T(8,128)(2,1)} %operator.1) | data formatting | bytes 131072

commit v3 on v2

--- a/solution.py
+++ b/solution.py
@@ -7,7 +7,9 @@
 
 MESH = pl.DeviceIdType.MESH
 SUBS = 4
-MOVE, SPREAD, FORWARD = (2, 8), (4, 9), (6, 10)
+MOVE, SPREAD, FORWARD = (2, 3, 8), (4, 5, 9), (6, 7, 10)
+START = (0, 0, 3)
+PIECES = ((1, 1), (2, 1), (0, 1))
 BRANCHES = ((1, 2), (0, 1))
 
 
@@ -158,7 +160,7 @@
     pl.semaphore_wait(barrier, len(met))
 
     def one_copy(h, p, landed=None):
-        some = pl.ds(*BRANCHES[p])
+        some = pl.ds(*PIECES[p])
         at = c if landed is None else landed
         src = w_ref.at[some, :, pl.ds(h * 128, 128)]
         return remote(src, stage_buf.at[at, some], one_s.at[h, p], one_r.at[at, p], one_to[h])
@@ -173,7 +175,9 @@
             def _():
                 one_copy(h, p).start()
 
-    set_out(0)
+    for p in range(3):
+        if START[p] == 0:
+            set_out(p)
 
     rows = 128 // SUBS
 
@@ -185,28 +189,24 @@
         dst = a_buf.at[held(way, t), c, part]
         src = tok_ref.at[part] if t == 0 else dst
         to = z_up if way == 0 else z_down
-        return remote(src, dst, ring_s.at[way, t, u], ring_r.at[way, t, u], to)
+        return remote(src, dst, ring_s.at[0], ring_r.at[way, t, u], to)
 
     def sib_copy(way, t):
         part = pl.ds(0, 128) if t < 8 else pl.ds(64 * way, 64)
         dst = a_buf.at[held(way, t), c, part]
         src = tok_ref if t == 0 else dst
-        return remote(src, dst, sib_s.at[way, t], sib_r.at[way, t], sibling)
+        return remote(src, dst, sib_s.at[0], sib_r.at[0], sibling)
 
     def uses(way, t):
         if t < 7:
             return range(SUBS)
         return range(SUBS // 2) if way == 0 else range(SUBS // 2, SUBS)
 
-    sent, sib_sent = [], []
     for u in range(SUBS):
         for way in range(2):
             copy = ring_copy(way, 0, u)
             copy.start()
-            sent.append(copy)
-    copy = sib_copy(0, 0)
-    copy.start()
-    sib_sent.append(copy)
+    sib_copy(0, 0).start()
 
     prm_copy = remote(prm_send, prm_buf, prm_s.at[0], prm_r.at[0], partner)
 
@@ -227,10 +227,10 @@
 
     def block(index, p):
         at = pl.ds(pl.multiple_of(index * 256, 256), 256)
-        return w_buf.at[pl.ds(*BRANCHES[p]), at]
+        return w_buf.at[pl.ds(*PIECES[p]), at]
 
     def two_copy(h, p):
-        src = stage_buf.at[h, pl.ds(*BRANCHES[p])]
+        src = stage_buf.at[h, pl.ds(*PIECES[p])]
         return remote(src, block(zl, p), two_s.at[h, p], two_r.at[zl // 4, p], two_to[h])
 
     def two_stays(h):
@@ -243,7 +243,7 @@
 
         @pl.when(two_stays(h))
         def _():
-            low, count = BRANCHES[p]
+            low, count = PIECES[p]
             at = pl.ds(pl.multiple_of(zl * 256, 256), 256)
             for b in range(low, low + count):
                 w_buf[b, at, :] = stage_buf[h, b]
@@ -256,25 +256,21 @@
         step = hop if way == 0 else -hop
         ref = block((first + 4 - step) % 4 + 4 * h, p)
         to = y_up if way == 0 else y_down
-        return remote(ref, ref, col_s.at[way, hop, h, p], col_r.at[way, hop, h, p], to)
+        return remote(ref, ref, col_s.at[0], col_r.at[way, hop, h, p], to)
 
     def spread(h, p):
         @pl.when(zl != first + 4 * h)
         def _():
-            src = stage_buf.at[h, pl.ds(*BRANCHES[p])]
+            src = stage_buf.at[h, pl.ds(*PIECES[p])]
             dst = block(first + 4 * h, p)
             remote(src, dst, two_s.at[h, p], two_r.at[h, p], two_to[h]).wait_recv()
 
         for way in range(2):
-            copy = col_copy(way, 0, h, p)
-            copy.start()
-            sent.append(copy)
+            col_copy(way, 0, h, p).start()
 
     def forward(way, p):
         col_copy(way, 0, way, p).wait_recv()
-        copy = col_copy(way, 1, way, p)
-        copy.start()
-        sent.append(copy)
+        col_copy(way, 1, way, p).start()
 
     def gathered(p):
         for way in range(2):
@@ -282,12 +278,12 @@
             col_copy(way, 1, way, p).wait_recv()
 
     def weights_at(t):
-        for p in range(2):
+        for p in range(3):
             for h in range(2):
                 if t == MOVE[p]:
                     move(h, p)
-            if t == MOVE[0] and p == 0:
-                set_out(1)
+            if t == START[p]:
+                set_out(p)
             for h in range(2):
                 if t == SPREAD[p]:
                     spread(h, p)
@@ -320,23 +316,22 @@
                     if t < 8 and u in uses(way, t):
                         copy = ring_copy(way, t, u)
                         copy.start()
-                        sent.append(copy)
         for way in range(2):
-            copy = sib_copy(way, t)
-            copy.start()
-            sib_sent.append(copy)
+            sib_copy(way, t).start()
         weights_at(t)
         if t == 5:
             modes()
     gathered(0)
-    for copy in sib_sent:
-        copy.wait_recv()
+    gathered(1)
+    shards_of = a_buf.at[:, 0]
+    sib_all = remote(shards_of, shards_of, sib_s.at[0], sib_r.at[0], sibling)
+    sib_all.wait_recv()
 
     def sum_copy(p, k):
         part, to_buf = ((part_kv, sum_kv), (part_q, sum_q))[p]
         to = (x + 1 + k) % 4
         return remote(
-            part.at[k], to_buf.at[k], sum_s.at[p, k], sum_r.at[p, k], device(to, y, z, c)
+            part.at[k], to_buf.at[k], sum_s.at[p], sum_r.at[p], device(to, y, z, c)
         )
 
     def product(p, to):
@@ -353,6 +348,10 @@
                 total = term if total is None else total + term
         return total
 
+    def sum_all(p):
+        part, to_buf = ((part_kv, sum_kv), (part_q, sum_q))[p]
+        return remote(part, to_buf, sum_s.at[p], sum_r.at[p], plane[1])
+
     lanes_of = (slice(128, 384), slice(0, 128))
 
     def products(p):
@@ -377,8 +376,8 @@
     def collect(p):
         got = (sum_kv, sum_q)[p]
         total = ext_buf[8:264, lanes_of[p]]
+        sum_all(p).wait_recv()
         for k in range(3):
-            sum_copy(p, k).wait_recv()
             total += got[k].astype(jnp.float32)
         rounded = total.astype(jnp.bfloat16)
         halo_send[:, lanes_of[p]] = rounded[240:256, :]
@@ -408,6 +407,7 @@
     products(0)
     weights_at(8 + 1)
     collect(0)
+    weights_at(8 + 2)
     join(0)
     gated_buf[...] = (mixed(1) * mixed(2)).astype(jnp.bfloat16).astype(jnp.float32)
 
@@ -431,17 +431,17 @@
 
     def state_copy(i):
         here = state_buf.at[mine]
-        return remote(here, here, st_s.at[i], st_r.at[i], plane[i])
+        return remote(here, here, st_s.at[0], st_r.at[0], plane[i])
 
     for i in range(1, 16):
         state_copy(i).start()
 
-    weights_at(8 + 2)
-    gathered(1)
+    gathered(2)
     products(1)
 
-    for i in range(1, 16):
-        state_copy(i).wait_recv()
+    others = state_buf.at[pl.ds(0, 15)]
+    state_all = remote(others, others, st_s.at[0], st_r.at[0], plane[1])
+    state_all.wait_recv()
     state = prm_buf[24:40, :]
     for m in range(15):
         state = jnp.where(m < mine, decay_256 * state + state_buf[m], state)
@@ -486,9 +486,12 @@
         def _():
             home_copy(q).start()
 
-    for copy in sent + sib_sent:
-        copy.wait_send()
-    for p in range(2):
+    all_but_one = a_buf.at[pl.ds(0, 15), 0]
+    remote(all_but_one, all_but_one, ring_s.at[0], ring_r.at[0, 0, 0], z_up).wait_send()
+    sib_all.wait_send()
+    col_all = w_buf.at[:, pl.ds(0, 1536)]
+    remote(col_all, col_all, col_s.at[0], col_r.at[0, 0, 0, 0], y_up).wait_send()
+    for p in range(3):
         for h in range(2):
 
             @pl.when(jnp.logical_not(one_stays(h)))
@@ -499,16 +502,15 @@
             def _():
                 two_copy(h, p).wait_send()
 
-        for k in range(3):
-            sum_copy(p, k).wait_send()
+    for p in range(2):
+        sum_all(p).wait_send()
         halo_copy(p).wait_send()
 
     @pl.when(away)
     def _():
         prm_copy.wait_send()
 
-    for i in range(1, 16):
-        state_copy(i).wait_send()
+    state_all.wait_send()
     for q in range(2):
 
         @pl.when(jnp.logical_not(jnp.logical_and(at_home, c == q)))
@@ -565,20 +567,20 @@
             pltpu.VMEM((16, 384), bf16),
             pltpu.VMEM((2, 128, 128), bf16),
             pltpu.VMEM((2, 128, 128), bf16),
+            dma((1,)),
             dma((2, 8, SUBS)),
-            dma((2, 8, SUBS)),
-            dma((2, 9)),
-            dma((2, 9)),
-            dma((2, 2)),
-            dma((2, 2)),
-            dma((2, 2)),
-            dma((2, 2)),
-            dma((2, 2, 2, 2)),
-            dma((2, 2, 2, 2)),
+            dma((1,)),
+            dma((1,)),
             dma((2, 3)),
             dma((2, 3)),
-            dma((16,)),
-            dma((16,)),
+            dma((2, 3)),
+            dma((2, 3)),
+            dma((1,)),
+            dma((2, 2, 2, 3)),
+            dma((2,)),
+            dma((2,)),
+            dma((1,)),
+            dma((1,)),
             dma((1,)),
             dma((1,)),
             dma((2,)),

time: 94.4 us -> 91.3 us (0.967)
  Pallas kernels: 92.8 us -> 89.6 us
    pallas_call x1, Pallas kernels: 92.8 us -> 89.6 us  [shards(): pl.pallas_call(kernel, out_shape=jax.ShapeDtypeStruct((128, 256), bf16),...]
where the time goes in v3:
time: 91.3 us; the launch traced here: 91.1 us
  Pallas kernels  89.6 us (98%)
  local copies, waits for them, and re-layouts  1.47 us (2%)
    pallas_call x1, Pallas kernels, shards(): pl.pallas_call(kernel, out_shape=jax.ShapeDtypeStruct((128, 256), bf16),...  89.6 us

profile of v3, /device:TPU:7, one launch (start us, length us, event | category | flops | bytes accessed | tf_op | source)
XLA Modules:
  0.0 91.1 jit_solution(10054227125254294958)
XLA Ops:
  0.0 89.6 %operator.1 = bf16[128,256]{1,0:T(8,128)(2,1)} custom-call(bf16[128,512]{1,0:T(8,128)(2,1)} %tok_in.1, bf16[3,256,256]{2,1,0:T(8,128)(2,1)} %bitcast.5, f32[3,3,256]{2,1,0:T(4,128)} %taps_in.1, bf16[3,2,256]{2,1,0:T(2,128)(2,1)} %bitcast.7, f32[16,16]{1,0:T(8,128)} %pole_in.1, f32[16,16]{1,0:T(8,128)} %res_in.1, f32[16,256]{1,0:T(8,128)} %bitcast.6, ...), custom_call_target="tpu_custom_call" | custom-call | tf_op jit(solution)/shard_map/operator/pallas_call | solution.py:544
  89.6 1.5 %copy.11 = bf16[128,256]{1,0:T(8,128)(2,1)} copy(bf16[128,256]{1,0:T(8,128)(2,1)} %operator.1) | data formatting | bytes 131072

commit v4 on v3

--- a/solution.py
+++ b/solution.py
@@ -11,6 +11,10 @@
 START = (0, 0, 3)
 PIECES = ((1, 1), (2, 1), (0, 1))
 BRANCHES = ((1, 2), (0, 1))
+
+
+def offset(pair):
+    return pair // 2 * (pair - 2) + (1 - pair // 2) * (3 - pair)
 
 
 def device(x, y, z, c):
@@ -121,9 +125,9 @@
     two_to = [device(x, y, zh * 8 + 2 * turn + h, c) for h in range(2)]
     first = (zl // 2 + x + y) % 4
     two_from = [device(x, y, zh * 8 + first + 4 * h, c) for h in range(2)]
-    own = (x + zl // 2) % 4
+    own = (x + offset(zl // 2)) % 4
     home_to = [device(zl // 2, y, zh * 8 + 2 * own + q, zl % 2) for q in range(2)]
-    owner = (zl // 2 + 4 - x) % 4
+    owner = (zl // 2 + 4 - offset(x)) % 4
     home_from = [device(owner, y, zh * 8 + 2 * x + c, h) for h in range(2)]
     partner = device(owner, y, zh * 8 + 2 * x + c, zl % 2)
     at_home = jnp.logical_and(zl // 2 == x, zl == 2 * own + c)
@@ -339,7 +343,7 @@
         for side in range(2):
             for core in range(2):
                 at = slice((side * 4 + core * 2) * 256, (side * 4 + core * 2) * 256 + 512)
-                left = a_buf[pl.ds(side * 8 + 2 * ((to + zl // 2) % 4), 2), core].reshape(256, 512)
+                left = a_buf[pl.ds(side * 8 + 2 * ((to + offset(zl // 2)) % 4), 2), core].reshape(256, 512)
                 if p == 0:
                     right = jnp.concatenate([w_buf[1, at, :], w_buf[2, at, :]], axis=1)
                 else:

time: 91.3 us -> 90.1 us (0.987)
  Pallas kernels: 89.6 us -> 88.4 us
    pallas_call x1, Pallas kernels: 89.6 us -> 88.4 us  [shards(): pl.pallas_call(kernel, out_shape=jax.ShapeDtypeStruct((128, 256), bf16),...]
where the time goes in v4:
time: 90.1 us; the launch traced here: 89.9 us
  Pallas kernels  88.4 us (98%)
  local copies, waits for them, and re-layouts  1.47 us (2%)
    pallas_call x1, Pallas kernels, shards(): pl.pallas_call(kernel, out_shape=jax.ShapeDtypeStruct((128, 256), bf16),...  88.4 us

profile of v4, /device:TPU:7, one launch (start us, length us, event | category | flops | bytes accessed | tf_op | source)
XLA Modules:
  0.0 89.9 jit_solution(6736105804116249914)
XLA Ops:
  0.0 88.4 %operator.1 = bf16[128,256]{1,0:T(8,128)(2,1)} custom-call(bf16[128,512]{1,0:T(8,128)(2,1)} %tok_in.1, bf16[3,256,256]{2,1,0:T(8,128)(2,1)} %bitcast.5, f32[3,3,256]{2,1,0:T(4,128)} %taps_in.1, bf16[3,2,256]{2,1,0:T(2,128)(2,1)} %bitcast.7, f32[16,16]{1,0:T(8,128)} %pole_in.1, f32[16,16]{1,0:T(8,128)} %res_in.1, f32[16,256]{1,0:T(8,128)} %bitcast.6, ...), custom_call_target="tpu_custom_call" | custom-call | tf_op jit(solution)/shard_map/operator/pallas_call | solution.py:548
  88.4 1.5 %copy.11 = bf16[128,256]{1,0:T(8,128)(2,1)} copy(bf16[128,256]{1,0:T(8,128)(2,1)} %operator.1) | data formatting | bytes 131072

commit v5 on v4

--- a/solution.py
+++ b/solution.py
@@ -135,8 +135,8 @@
     one_same = jnp.logical_and(x == y, turn == y)
 
     barrier = pltpu.get_barrier_semaphore()
-    met = [z_up, z_down, sibling] + plane[1:] + one_to + one_from + two_to + two_from
-    met = met + home_to + home_from
+    met = home_to + home_from + two_to + two_from + one_to + one_from + plane[:0:-1]
+    met = met + [z_up, z_down, sibling]
     for other in met:
         pl.semaphore_signal(barrier, inc=1, device_id=other, device_id_type=MESH)
 
@@ -361,8 +361,9 @@
     def products(p):
         part = (part_kv, part_q)[p]
 
-        @pl.loop(0, 3)
-        def _(k):
+        @pl.loop(1, 4)
+        def _(turned):
+            k = turned % 3
             part[k] = product(p, (x + 1 + k) % 4).astype(jnp.bfloat16)
             sum_copy(p, k).start()
 

time: 90.1 us -> 89.2 us (0.990)
  Pallas kernels: 88.4 us -> 87.1 us
    pallas_call x1, Pallas kernels: 88.4 us -> 87.1 us  [shards(): pl.pallas_call(kernel, out_shape=jax.ShapeDtypeStruct((128, 256), bf16),...]
where the time goes in v5:
time: 89.2 us; the launch traced here: 88.6 us
  Pallas kernels  87.1 us (98%)
  local copies, waits for them, and re-layouts  1.47 us (2%)
    pallas_call x1, Pallas kernels, shards(): pl.pallas_call(kernel, out_shape=jax.ShapeDtypeStruct((128, 256), bf16),...  87.1 us

profile of v5, /device:TPU:7, one launch (start us, length us, event | category | flops | bytes accessed | tf_op | source)
XLA Modules:
  0.0 88.6 jit_solution(16525753995803839020)
XLA Ops:
  0.0 87.1 %operator.1 = bf16[128,256]{1,0:T(8,128)(2,1)} custom-call(bf16[128,512]{1,0:T(8,128)(2,1)} %tok_in.1, bf16[3,256,256]{2,1,0:T(8,128)(2,1)} %bitcast.5, f32[3,3,256]{2,1,0:T(4,128)} %taps_in.1, bf16[3,2,256]{2,1,0:T(2,128)(2,1)} %bitcast.7, f32[16,16]{1,0:T(8,128)} %pole_in.1, f32[16,16]{1,0:T(8,128)} %res_in.1, f32[16,256]{1,0:T(8,128)} %bitcast.6, ...), custom_call_target="tpu_custom_call" | custom-call | tf_op jit(solution)/shard_map/operator/pallas_call | solution.py:549
  87.1 1.5 %copy.11 = bf16[128,256]{1,0:T(8,128)(2,1)} copy(bf16[128,256]{1,0:T(8,128)(2,1)} %operator.1) | data formatting | bytes 131072

commit v6 on v5

--- a/solution.py
+++ b/solution.py
@@ -179,9 +179,6 @@
             def _():
                 one_copy(h, p).start()
 
-    for p in range(3):
-        if START[p] == 0:
-            set_out(p)
 
     rows = 128 // SUBS
 
@@ -212,6 +209,9 @@
             copy.start()
     sib_copy(0, 0).start()
 
+    for p in range(3):
+        if START[p] == 0:
+            set_out(p)
     prm_copy = remote(prm_send, prm_buf, prm_s.at[0], prm_r.at[0], partner)
 
     @pl.when(away)

time: 89.2 us -> 89.2 us (level)
  no operation moved by 1% of the time
where the time goes in v6:
time: 89.2 us; the launch traced here: 88.6 us
  Pallas kernels  87.1 us (98%)
  local copies, waits for them, and re-layouts  1.47 us (2%)
    pallas_call x1, Pallas kernels, shards(): pl.pallas_call(kernel, out_shape=jax.ShapeDtypeStruct((128, 256), bf16),...  87.1 us

profile of v6, /device:TPU:7, one launch (start us, length us, event | category | flops | bytes accessed | tf_op | source)
XLA Modules:
  0.0 88.6 jit_solution(13008171600497325119)
XLA Ops:
  0.0 87.1 %operator.1 = bf16[128,256]{1,0:T(8,128)(2,1)} custom-call(bf16[128,512]{1,0:T(8,128)(2,1)} %tok_in.1, bf16[3,256,256]{2,1,0:T(8,128)(2,1)} %bitcast.5, f32[3,3,256]{2,1,0:T(4,128)} %taps_in.1, bf16[3,2,256]{2,1,0:T(2,128)(2,1)} %bitcast.7, f32[16,16]{1,0:T(8,128)} %pole_in.1, f32[16,16]{1,0:T(8,128)} %res_in.1, f32[16,256]{1,0:T(8,128)} %bitcast.6, ...), custom_call_target="tpu_custom_call" | custom-call | tf_op jit(solution)/shard_map/operator/pallas_call | solution.py:549
  87.1 1.5 %copy.11 = bf16[128,256]{1,0:T(8,128)(2,1)} copy(bf16[128,256]{1,0:T(8,128)(2,1)} %operator.1) | data formatting | bytes 131072
